TPU v7x, 32 devices: a whole 2x2x4 slice. The times are simulated.
32 devices in a mesh: grp: 2 (over y), row: 4 (over z), col: 4 (over x, core).
Axes of the slice: x: 2, y: 2, z: 4, core: 2. Of those that a mesh axis runs over, the one named last changes fastest.
Arguments:
- inputs: bfloat16 [256, 16384], P(('grp', 'row'), 'col'), parts along dimension 0, may hold values from -6 to 6
- output_gradient: bfloat16 [256, 16384], P(('grp', 'row'), 'col'), parts along dimension 0, may hold values from -6 to 6
- gate_preactivation: bfloat16 [256, 8192], P('grp', 'row'), parts along dimension 0, may hold values from -6 to 6
- up_preactivation: bfloat16 [256, 8192], P('grp', 'row'), parts along dimension 0, may hold values from -6 to 6
- gate_weight: bfloat16 [16384, 8192], P('col', 'row'), may hold values from -0.046875 to 0.046875
- up_weight: bfloat16 [16384, 8192], P('col', 'row'), may hold values from -0.046875 to 0.046875
- down_weight: bfloat16 [8192, 16384], P('row', 'col'), may hold values from -0.0625 to 0.0625
- up_adapter_entry: bfloat16 [16, 16384], P(None, 'col'), may hold values from -6 to 6
- up_adapter_exit: bfloat16 [16, 8192], P(None, 'row'), may hold values from -0.0032958984 to 0.0032958984
- down_adapter_entry: bfloat16 [16, 8192], P(None, 'row'), may hold values from -6 to 6
- down_adapter_exit: bfloat16 [16, 16384], P(None, 'col'), may hold values from -0.0023956299 to 0.0023956299
- up_adapter_activations: bfloat16 [16, 256], P(None, 'grp'), parts along dimension 1, may hold values from -0.29882812 to 0.29882812
- down_adapter_activations: bfloat16 [16, 256], P(None, 'grp'), parts along dimension 1, may hold values from -0.29882812 to 0.29882812
Outputs:
- grad_inputs: bfloat16 [256, 16384], P(('grp', 'row'), 'col'), parts along dimension 0
- up_entry_gradient: float32 [32, 16384], P('grp', 'col'), parts along dimension 0
- up_exit_gradient: float32 [32, 8192], P('grp', 'row'), parts along dimension 0
- down_entry_gradient: float32 [32, 8192], P('grp', 'row'), parts along dimension 0
- down_exit_gradient: float32 [32, 16384], P('grp', 'col'), parts along dimension 0
There are 2 independent parts, one for each index of `grp`. A program takes and returns all parts, laid end to end along the dimension named above; an argument that names none is the same for every part. Nothing has to cross between parts.
All inputs are finite; a program needn't handle non-finite values.
Results may differ from a plain program's by a relative error of at most 0.005.
Values may be sent and summed in bfloat16 or wider, within the bound.
No kernel may reach another device: no remote copies, remote signals or barrier semaphores. Data moves between devices by JAX's collectives and lax.ppermute only.
A program may use at most 128 MiB of HBM per device.

v0:
```python
import jax
import jax.numpy as jnp
from jax import lax
from jax.sharding import PartitionSpec as P

adapter_scale = 2.0


def contract_trailing(left, right):
    return lax.dot_general(
        left, right, (((1,), (1,)), ((), ())), preferred_element_type=jnp.float32
    )


def contract_leading(left, right, matmul_accuracy=None):
    return lax.dot_general(
        left,
        right,
        (((0,), (0,)), ((), ())),
        precision=matmul_accuracy,
        preferred_element_type=jnp.float32,
    )


def body(
    inputs,
    output_gradient,
    gate_preactivation,
    up_preactivation,
    gate_weight,
    up_weight,
    down_weight,
    up_adapter_entry,
    up_adapter_exit,
    down_adapter_entry,
    down_adapter_exit,
    up_adapter_activations,
    down_adapter_activations,
):
    highest_setting = lax.Precision.HIGHEST
    complete_gradient = lax.all_gather(output_gradient, "row", axis=0, tiled=True)
    down_piece = contract_trailing(complete_gradient, down_adapter_exit)
    hidden_piece = contract_trailing(complete_gradient, down_weight)
    hidden_piece = hidden_piece + adapter_scale * jnp.dot(
        down_piece, down_adapter_entry.astype(jnp.float32), precision=highest_setting
    )
    hidden_gradient, down_full = lax.psum((hidden_piece, down_piece), "col")
    gate_f = gate_preactivation.astype(jnp.float32)
    up_f = up_preactivation.astype(jnp.float32)
    sigmoid_gate = jax.nn.sigmoid(gate_f)
    hidden_state = (gate_f * sigmoid_gate * up_f).astype(jnp.bfloat16)
    gate_grad = (
        hidden_gradient * up_f * sigmoid_gate * (1.0 + gate_f * (1.0 - sigmoid_gate))
    ).astype(jnp.bfloat16)
    up_gradient = (hidden_gradient * gate_f * sigmoid_gate).astype(jnp.bfloat16)
    down_rounded_value = down_full.astype(jnp.bfloat16)
    upper_piece = contract_trailing(up_gradient, up_adapter_exit)
    input_piece = contract_trailing(gate_grad, gate_weight) + contract_trailing(
        up_gradient, up_weight
    )
    input_piece = input_piece + adapter_scale * jnp.dot(
        upper_piece, up_adapter_entry.astype(jnp.float32), precision=highest_setting
    )
    input_grad, upper_full = (
        lax.psum_scatter(input_piece, "row", scatter_dimension=0, tiled=True),
        lax.psum_scatter(upper_piece, "row", scatter_dimension=0, tiled=True),
    )
    up_entry_term = adapter_scale * contract_leading(
        upper_full, inputs.astype(jnp.float32), matmul_accuracy=highest_setting
    )
    up_entry_gradient = lax.psum(up_entry_term, "row")
    up_exit_gradient = adapter_scale * jnp.dot(
        up_adapter_activations, up_gradient, preferred_element_type=jnp.float32
    )
    down_entry_gradient = adapter_scale * contract_leading(down_rounded_value, hidden_state)
    down_exit_gradient = adapter_scale * jnp.dot(
        down_adapter_activations, complete_gradient, preferred_element_type=jnp.float32
    )
    return (
        input_grad.astype(jnp.bfloat16),
        up_entry_gradient,
        up_exit_gradient,
        down_entry_gradient,
        down_exit_gradient,
    )


def solution(mesh):
    placed = (
        P(("grp", "row"), "col"),
        P(("grp", "row"), "col"),
        P("grp", "row"),
        P("grp", "row"),
        P("col", "row"),
        P("col", "row"),
        P("row", "col"),
        P(None, "col"),
        P(None, "row"),
        P(None, "row"),
        P(None, "col"),
        P(None, "grp"),
        P(None, "grp"),
    )
    return jax.shard_map(
        body,
        mesh=mesh,
        in_specs=placed,
        out_specs=(
            P(("grp", "row"), "col"),
            P("grp", "col"),
            P("grp", "row"),
            P("grp", "row"),
            P("grp", "col"),
        ),
        check_vma=False,
    )
```

profile of v0, /device:TPU:0, one launch (start us, length us, event | category | flops | bytes accessed | tf_op | source)
XLA Modules:
  0.0 212.7 jit_solution(2744428697788110122)
XLA Ops:
  7.3 0.7 all-gather.2.cloned.1.call-update
  8.0 32.3 %all-gather.2.cloned.1.call-done = bf16[128,4096]{1,0:T(8,128)(2,1)} async-done(((bf16[32,4096]{1,0:T(8,128)(2,1)}), bf16[128,4096]{1,0:T(8,128)(2,1)}) %all-gather.2.cloned.1.call-update) | async-done | bytes 1048592 | tf_op jit(solution)/shard_map/all_gather | solution.py:41
  40.3 1.6 fusion.21
  41.9 11.8 %fusion.20 = f32[128,2048]{1,0:T(8,128)S(1)} fusion(bf16[128,4096]{1,0:T(8,128)(2,1)} %all-gather.2.cloned.1.call-done, bf16[2048,4096]{1,0:T(8,128)(2,1)} %param.19), kind=kOutput, calls=%fused_computation.31 | convolution fusion | flops 2147483648 | bytes 18874368 | tf_op jit(solution)/shard_map/dot_general | solution.py:10
  53.7 1.6 fusion.1
  55.3 35.7 %all-reduce.3.cloned.1.call-done = f32[128,2048]{1,0:T(8,128)} async-done(((f32[128,2048]{1,0:T(8,128)}), f32[128,2048]{1,0:T(8,128)}) %all-reduce.3.cloned.1.call-update) | async-done | bytes 1048592 | tf_op jit(solution)/shard_map/psum | solution.py:47
  91.0 1.5 fusion.12
  92.5 0.8 copy-done.2
  93.3 0.2 fusion.22
  93.6 0.8 copy.18
  94.4 0.2 reduce-scatter.5.cloned.1.call-start
  94.6 13.2 %fusion.13 = f32[128,4096]{1,0:T(8,128)} fusion(bf16[4096,2048]{1,0:T(8,128)(2,1)} %param.17, f32[128,2048]{1,0:T(8,128)} %all-reduce.3.cloned.1.call-done, bf16[128,2048]{1,0:T(8,128)(2,1)S(1)} %copy-done.7, bf16[128,2048]{1,0:T(8,128)(2,1)S(1)} %copy-done.3), kind=kOutput, calls=%fused_computation.26 | convolution fusion | flops 2150629376 | bytes 20971520 | tf_op jit(solution)/shard_map/dot_general | solution.py:10
  107.8 12.3 %convolution_add_fusion = f32[128,4096]{1,0:T(8,128)S(1)} fusion(f32[128,4096]{1,0:T(8,128)} %fusion.13, bf16[128,2048]{1,0:T(8,128)(2,1)} %copy-done.2, bf16[4096,2048]{1,0:T(8,128)(2,1)} %param.18), kind=kOutput, calls=%fused_computation.2 | convolution fusion | flops 2148007936 | bytes 21495808 | tf_op jit(solution)/shard_map/dot_general | solution.py:10
  120.1 2.4 %fusion = f32[128,4096]{1,0:T(8,128)} fusion(f32[128,4096]{1,0:T(8,128)S(1)} %convolution_add_fusion, f32[128,16]{0,1:T(8,128)S(1)} %fusion.22, bf16[16,4096]{1,0:T(8,128)(2,1)S(1)} %copy-done.4), kind=kOutput, calls=%fused_computation.1 | convolution fusion | flops 101711872 | bytes 4333568 | tf_op jit(solution)/shard_map/dot_general | solution.py:61
  122.5 0.0 all-reduce.5.cloned.1.call-start
  122.6 6.0 %psum.23 = bf16[128,16]{0,1:T(8,128)(2,1)S(1)} all-reduce(f32[128,16]{0,1:T(8,128)S(1)} %fusion.21), channel_id=1, replica_groups=mesh['grp'=2,'row'=4,'col'=4] {'col'}, use_global_device_ids=true, to_apply=%region_4.0 | all-reduce | flops 2048 | bytes 12288 | tf_op jit(solution)/shard_map/psum | solution.py:47
  128.6 2.4 %convolution_multiply_fusion.5 = f32[16,2048]{1,0:T(8,128)} fusion(bf16[128,2048]{1,0:T(8,128)(2,1)} %param.16, bf16[128,2048]{1,0:T(8,128)(2,1)} %param.15, bf16[128,16]{0,1:T(8,128)(2,1)S(1)} %psum.23), kind=kOutput, calls=%fused_computation.9 | convolution fusion | flops 10518528 | bytes 1183744 | tf_op jit(solution)/shard_map/dot_general | solution.py:16
  131.0 1.7 convolution_multiply_fusion.2
  132.8 1.6 convolution_multiply_fusion.1
  134.4 1.9 fusion.2
  136.3 30.6 %reduce-scatter.5.cloned.1.call-done = f32[32,4096]{1,0:T(8,128)} async-done(((f32[128,4096]{1,0:T(8,128)}), f32[32,4096]{1,0:T(8,128)}) %reduce-scatter.5.cloned.1.call-update) | async-done | bytes 524304 | tf_op jit(solution)/shard_map/reduce_scatter | solution.py:65
  166.9 1.8 convert_element_type.28
  168.7 35.8 %all-reduce.5.cloned.1.call-done = f32[16,4096]{1,0:T(8,128)} async-done(((f32[16,4096]{1,0:T(8,128)}), f32[16,4096]{1,0:T(8,128)}) %all-reduce.5.cloned.1.call-update) | async-done | bytes 262160 | tf_op jit(solution)/shard_map/psum | solution.py:71
  204.5 1.7 copy.22
  (23 shorter events, 0.2 us)
Async XLA Ops:
  7.2 123.8 %copy-start = (bf16[32,4096]{1,0:T(8,128)(2,1)S(1)}, bf16[32,4096]{1,0:T(8,128)(2,1)}, u32[]{:S(2)}) copy-start(bf16[32,4096]{1,0:T(8,128)(2,1)} %param.13) | copy-start | bytes 786436
  7.2 46.5 %copy-start.5 = (bf16[16,2048]{1,0:T(8,128)(2,1)S(1)}, bf16[16,2048]{1,0:T(8,128)(2,1)}, u32[]{:S(2)}) copy-start(bf16[16,2048]{1,0:T(8,128)(2,1)} %param.22) | copy-start | bytes 196612
  7.2 83.8 %copy-start.3 = (bf16[128,2048]{1,0:T(8,128)(2,1)S(1)}, bf16[128,2048]{1,0:T(8,128)(2,1)}, u32[]{:S(2)}) copy-start(bf16[128,2048]{1,0:T(8,128)(2,1)} %param.15) | copy-start | bytes 1572868
  7.2 86.1 %copy-start.6 = (bf16[16,2048]{1,0:T(8,128)(2,1)S(1)}, bf16[16,2048]{1,0:T(8,128)(2,1)}, u32[]{:S(2)}) copy-start(bf16[16,2048]{1,0:T(8,128)(2,1)} %param.21) | copy-start | bytes 196612
  7.2 87.4 %copy-start.7 = (bf16[128,2048]{1,0:T(8,128)(2,1)S(1)}, bf16[128,2048]{1,0:T(8,128)(2,1)}, u32[]{:S(2)}) copy-start(bf16[128,2048]{1,0:T(8,128)(2,1)} %param.16) | copy-start | bytes 1572868
  7.2 33.1 %all-gather.2.cloned.1.call-start = ((), (), s32[]{:S(2)}) async-start(), calls=%async_computation.2 | async-start | bytes 1310720 | tf_op jit(solution)/shard_map/all_gather | solution.py:41
  8.0 83.1 %all-reduce.3.cloned.1.call-start = ((), (), s32[]{:S(2)}) async-start(), calls=%async_computation.3 | async-start | bytes 2097152 | tf_op jit(solution)/shard_map/psum | solution.py:47
  55.3 75.7 %reduce-scatter.7.cloned.1.call-start = ((), (), s32[]{:S(2)}) async-start(), calls=%async_computation.6 | async-start | bytes 81920
  92.5 0.8 copy-start.2
  94.4 25.7 %copy-start.4 = (bf16[16,4096]{1,0:T(8,128)(2,1)S(1)}, bf16[16,4096]{1,0:T(8,128)(2,1)}, u32[]{:S(2)}) copy-start(bf16[16,4096]{1,0:T(8,128)(2,1)} %param.20) | copy-start | bytes 393220
  94.4 72.5 %reduce-scatter.5.cloned.1.call-start = ((), (), s32[]{:S(2)}) async-start(), calls=%async_computation.4 | async-start | bytes 2621440 | tf_op jit(solution)/shard_map/reduce_scatter | solution.py:65
  107.8 25.0 %copy-start.1 = (bf16[128,4096]{1,0:T(8,128)(2,1)S(1)}, bf16[128,4096]{1,0:T(8,128)(2,1)}, u32[]{:S(2)}) copy-start(bf16[128,4096]{1,0:T(8,128)(2,1)} %all-gather.2.cloned.1.call-done) | copy-start | bytes 3145732
  122.5 82.0 %all-reduce.5.cloned.1.call-start = ((), (), s32[]{:S(2)}) async-start(), calls=%async_computation.5 | async-start | bytes 524288 | tf_op jit(solution)/shard_map/psum | solution.py:71
Sparse Core Ops, SparseCore 0:
  9.6 30.6 all-gather.1
  55.4 35.5 all-reduce.2
  94.5 19.4 reduce-scatter.6
  122.6 44.2 reduce-scatter.4
  169.8 34.6 all-reduce.4
where the time goes:
time: 213 us
  waiting for transfers between devices  135 us (63%)
  matrix products  50.8 us (24%)
  between operations  13.9 us (7%)
  blocking collectives  6 us (3%)
  other arithmetic  3.28 us (2%)
  local copies, waits for them, and re-layouts  3.27 us (2%)
    dot_general x5, matrix products, contract_trailing(): lax.dot_general(left, right, (((1,), (1,)), ((), ())), preferred_element_...  39 us
    psum x1, waiting for transfers between devices, body(): up_entry_gradient = lax.psum(up_entry_term, 'row')  35.8 us
    psum x1, waiting for transfers between devices, body(): hidden_gradient, down_full = lax.psum((hidden_piece, down_piece), 'col')  35.7 us
    all_gather x1, waiting for transfers between devices, body(): lax.all_gather(output_gradient, 'row', axis=0, tiled=True)  32.3 us
    reduce_scatter x1, waiting for transfers between devices, body(): lax.psum_scatter(input_piece, 'row', scatter_dimension=0, tiled=True)  30.6 us
    psum x1, blocking collectives, body(): hidden_gradient, down_full = lax.psum((hidden_piece, down_piece), 'col')  6 us
  transfers between devices with their start and end apart: 5, of which 4 were waited for; matrix products, arithmetic and copies ran while one was open for 18% of the time, Pallas kernels for 0%

commit v1 on v0

--- a/solution.py
+++ b/solution.py
@@ -4,6 +4,11 @@
 from jax.sharding import PartitionSpec as P
 
 adapter_scale = 2.0
+
+
+def summed_here(x, name):
+    parts = lax.all_gather(x, name)
+    return jnp.sum(parts, axis=0)
 
 
 def contract_trailing(left, right):
@@ -68,7 +73,7 @@
     up_entry_term = adapter_scale * contract_leading(
         upper_full, inputs.astype(jnp.float32), matmul_accuracy=highest_setting
     )
-    up_entry_gradient = lax.psum(up_entry_term, "row")
+    up_entry_gradient = summed_here(up_entry_term, "row")
     up_exit_gradient = adapter_scale * jnp.dot(
         up_adapter_activations, up_gradient, preferred_element_type=jnp.float32
     )

time: 213 us -> 196 us (0.920)
  waiting for transfers between devices: 135 us -> 118 us
    psum x1 -> x0, waiting for transfers between devices: 35.8 us -> none  [body(): up_entry_gradient = lax.psum(up_entry_term, 'row')]
    unnamed x6, waiting for transfers between devices: 0.75 us -> 20.3 us
where the time goes in v1:
time: 196 us
  waiting for transfers between devices  118 us (60%)
  matrix products  50.9 us (26%)
  between operations  13.9 us (7%)
  blocking collectives  5.76 us (3%)
  other arithmetic  5.3 us (3%)
    dot_general x5, matrix products, contract_trailing(): lax.dot_general(left, right, (((1,), (1,)), ((), ())), preferred_element_...  39.3 us
    psum x1, waiting for transfers between devices, body(): hidden_gradient, down_full = lax.psum((hidden_piece, down_piece), 'col')  35.7 us
    all_gather x1, waiting for transfers between devices, body(): lax.all_gather(output_gradient, 'row', axis=0, tiled=True)  32.3 us
    reduce_scatter x1, waiting for transfers between devices, body(): lax.psum_scatter(input_piece, 'row', scatter_dimension=0, tiled=True)  29.9 us
    unnamed x6, waiting for transfers between devices  20.3 us
    psum x1, blocking collectives, body(): hidden_gradient, down_full = lax.psum((hidden_piece, down_piece), 'col')  5.76 us
    dot_general x2, matrix products, contract_leading(): lax.dot_general(left, right, (((0,), (0,)), ((), ())), precision=matmul_a...  4.02 us
  transfers between devices with their start and end apart: 5, of which 4 were waited for; matrix products, arithmetic and copies ran while one was open for 18% of the time, Pallas kernels for 0%

profile of v1, /device:TPU:0, one launch (start us, length us, event | category | flops | bytes accessed | tf_op | source)
XLA Modules:
  0.0 195.9 jit_solution(463190421693803917)
XLA Ops:
  7.3 0.7 all-gather.4.cloned.1.call-update
  8.0 32.3 %all-gather.4.cloned.1.call-done = bf16[128,4096]{1,0:T(8,128)(2,1)} async-done(((bf16[32,4096]{1,0:T(8,128)(2,1)}), bf16[128,4096]{1,0:T(8,128)(2,1)}) %all-gather.4.cloned.1.call-update) | async-done | bytes 1048592 | tf_op jit(solution)/shard_map/all_gather | solution.py:46
  40.3 1.6 fusion.21
  41.9 11.8 %fusion.20 = f32[128,2048]{1,0:T(8,128)S(1)} fusion(bf16[128,4096]{1,0:T(8,128)(2,1)} %all-gather.4.cloned.1.call-done, bf16[2048,4096]{1,0:T(8,128)(2,1)} %param.19), kind=kOutput, calls=%fused_computation.31 | convolution fusion | flops 2147483648 | bytes 18874368 | tf_op jit(solution)/shard_map/dot_general | solution.py:15
  53.7 1.6 fusion.1
  55.3 0.0 reduce-scatter.7.cloned.1.call-start
  55.4 35.7 %all-reduce.2.cloned.1.call-done = f32[128,2048]{1,0:T(8,128)} async-done(((f32[128,2048]{1,0:T(8,128)}), f32[128,2048]{1,0:T(8,128)}) %all-reduce.2.cloned.1.call-update) | async-done | bytes 1048592 | tf_op jit(solution)/shard_map/psum | solution.py:52
  91.0 1.5 fusion.12
  92.5 0.8 copy-done.2
  93.4 0.2 fusion.22
  93.6 0.8 copy.18
  94.4 19.5 %reduce-scatter.7.cloned.1.call-done = f32[32,16]{1,0:T(8,128)} async-done(((f32[128,16]{1,0:T(8,128)}), f32[32,16]{1,0:T(8,128)}) %reduce-scatter.7.cloned.1.call-update) | async-done | bytes 2064
  114.0 1.7 convolution_multiply_fusion.2
  115.7 0.2 reduce-scatter.5.cloned.1.call-start
  116.0 13.4 %fusion.13 = f32[128,4096]{1,0:T(8,128)} fusion(bf16[4096,2048]{1,0:T(8,128)(2,1)} %param.17, f32[128,2048]{1,0:T(8,128)} %all-reduce.2.cloned.1.call-done, bf16[128,2048]{1,0:T(8,128)(2,1)S(1)} %copy-done.7, bf16[128,2048]{1,0:T(8,128)(2,1)S(1)} %copy-done.3), kind=kOutput, calls=%fused_computation.26 | convolution fusion | flops 2150629376 | bytes 20971520 | tf_op jit(solution)/shard_map/dot_general | solution.py:15
  129.3 12.3 %convolution_add_fusion = f32[128,4096]{1,0:T(8,128)S(1)} fusion(f32[128,4096]{1,0:T(8,128)} %fusion.13, bf16[128,2048]{1,0:T(8,128)(2,1)} %copy-done.2, bf16[4096,2048]{1,0:T(8,128)(2,1)} %param.18), kind=kOutput, calls=%fused_computation.2 | convolution fusion | flops 2148007936 | bytes 21495808 | tf_op jit(solution)/shard_map/dot_general | solution.py:15
  141.7 2.4 %fusion = f32[128,4096]{1,0:T(8,128)} fusion(f32[128,4096]{1,0:T(8,128)S(1)} %convolution_add_fusion, f32[128,16]{0,1:T(8,128)S(1)} %fusion.22, bf16[16,4096]{1,0:T(8,128)(2,1)S(1)} %copy-done.4), kind=kOutput, calls=%fused_computation.1 | convolution fusion | flops 101711872 | bytes 4333568 | tf_op jit(solution)/shard_map/dot_general | solution.py:66
  144.1 5.8 %psum.15 = bf16[128,16]{0,1:T(8,128)(2,1)S(1)} all-reduce(f32[128,16]{0,1:T(8,128)S(1)} %fusion.21), channel_id=1, replica_groups=mesh['grp'=2,'row'=4,'col'=4] {'col'}, use_global_device_ids=true, to_apply=%region_4.0 | all-reduce | flops 2048 | bytes 12288 | tf_op jit(solution)/shard_map/psum | solution.py:52
  149.9 1.6 convolution_multiply_fusion.1
  151.5 2.3 %convolution_multiply_fusion.5 = f32[16,2048]{1,0:T(8,128)} fusion(bf16[128,2048]{1,0:T(8,128)(2,1)} %param.16, bf16[128,2048]{1,0:T(8,128)(2,1)} %param.15, bf16[128,16]{0,1:T(8,128)(2,1)S(1)} %psum.15), kind=kOutput, calls=%fused_computation.9 | convolution fusion | flops 10518528 | bytes 1183744 | tf_op jit(solution)/shard_map/dot_general | solution.py:21
  153.8 1.9 fusion.2
  155.7 2.0 %reduce_sum.9 = f32[16,4096]{1,0:T(8,128)} reduce(f32[4,16,4096]{2,1,0:T(8,128)} %bitcast.24, f32[]{:T(128)} %constant.5.clone.1), dimensions={0}, to_apply=%region_3.0 | reduce | flops 196608 | bytes 1310724 | tf_op jit(solution)/shard_map/reduce_sum | solution.py:11
  157.8 29.9 %reduce-scatter.5.cloned.1.call-done = f32[32,4096]{1,0:T(8,128)} async-done(((f32[128,4096]{1,0:T(8,128)}), f32[32,4096]{1,0:T(8,128)}) %reduce-scatter.5.cloned.1.call-update) | async-done | bytes 524304 | tf_op jit(solution)/shard_map/reduce_scatter | solution.py:70
  187.6 1.8 convert_element_type.28
  (23 shorter events, 0.2 us)
Async XLA Ops:
  7.2 106.8 %copy-start = (bf16[32,4096]{1,0:T(8,128)(2,1)S(1)}, bf16[32,4096]{1,0:T(8,128)(2,1)}, u32[]{:S(2)}) copy-start(bf16[32,4096]{1,0:T(8,128)(2,1)} %param.13) | copy-start | bytes 786436
  7.2 46.5 %copy-start.5 = (bf16[16,2048]{1,0:T(8,128)(2,1)S(1)}, bf16[16,2048]{1,0:T(8,128)(2,1)}, u32[]{:S(2)}) copy-start(bf16[16,2048]{1,0:T(8,128)(2,1)} %param.22) | copy-start | bytes 196612
  7.2 83.8 %copy-start.3 = (bf16[128,2048]{1,0:T(8,128)(2,1)S(1)}, bf16[128,2048]{1,0:T(8,128)(2,1)}, u32[]{:S(2)}) copy-start(bf16[128,2048]{1,0:T(8,128)(2,1)} %param.15) | copy-start | bytes 1572868
  7.2 86.2 %copy-start.6 = (bf16[16,2048]{1,0:T(8,128)(2,1)S(1)}, bf16[16,2048]{1,0:T(8,128)(2,1)}, u32[]{:S(2)}) copy-start(bf16[16,2048]{1,0:T(8,128)(2,1)} %param.21) | copy-start | bytes 196612
  7.2 108.8 %copy-start.7 = (bf16[128,2048]{1,0:T(8,128)(2,1)S(1)}, bf16[128,2048]{1,0:T(8,128)(2,1)}, u32[]{:S(2)}) copy-start(bf16[128,2048]{1,0:T(8,128)(2,1)} %param.16) | copy-start | bytes 1572868
  7.2 33.1 %all-gather.4.cloned.1.call-start = ((), (), s32[]{:S(2)}) async-start(), calls=%async_computation.2 | async-start | bytes 1310720 | tf_op jit(solution)/shard_map/all_gather | solution.py:46
  8.0 83.1 %all-reduce.2.cloned.1.call-start = ((), (), s32[]{:S(2)}) async-start(), calls=%async_computation.3 | async-start | bytes 2097152 | tf_op jit(solution)/shard_map/psum | solution.py:52
  55.3 58.6 %reduce-scatter.7.cloned.1.call-start = ((), (), s32[]{:S(2)}) async-start(), calls=%async_computation.6 | async-start | bytes 81920
  92.5 0.8 copy-start.2
  94.4 61.3 %all-gather.6.cloned.1.call-start = ((), (), s32[]{:S(2)}) async-start(), calls=%async_computation.5 | async-start | bytes 1310720 | tf_op jit(solution)/shard_map/all_gather | solution.py:10
  115.7 26.0 %copy-start.4 = (bf16[16,4096]{1,0:T(8,128)(2,1)S(1)}, bf16[16,4096]{1,0:T(8,128)(2,1)}, u32[]{:S(2)}) copy-start(bf16[16,4096]{1,0:T(8,128)(2,1)} %param.20) | copy-start | bytes 393220
  115.7 71.9 %reduce-scatter.5.cloned.1.call-start = ((), (), s32[]{:S(2)}) async-start(), calls=%async_computation.4 | async-start | bytes 2621440 | tf_op jit(solution)/shard_map/reduce_scatter | solution.py:70
  129.3 20.6 %copy-start.1 = (bf16[128,4096]{1,0:T(8,128)(2,1)S(1)}, bf16[128,4096]{1,0:T(8,128)(2,1)}, u32[]{:S(2)}) copy-start(bf16[128,4096]{1,0:T(8,128)(2,1)} %all-gather.4.cloned.1.call-done) | copy-start | bytes 3145732
Sparse Core Ops, SparseCore 0:
  9.6 30.6 all-gather.3
  55.4 35.5 all-reduce.1
  94.5 19.4 reduce-scatter.6
  116.0 26.3 all-gather.5
  144.5 43.0 reduce-scatter.4
